TPU v7x, 512 devices: a whole 4x4x16 slice. The times are simulated.
512 devices in a mesh: expert: 4 (over z_hi, core), rep: 4 (over y), hid: 32 (over x, z_lo).
Axes of the slice: x: 4, y: 4, z: 16 (z_hi: 2, z_lo: 8; z = z_hi * 8 + z_lo), core: 2. Of those that a mesh axis runs over, the one named last changes fastest.
Arguments:
- tokens: bfloat16 [1024, 6144], P(('expert', 'hid'), 'rep'), may hold values from -6 to 6
- norm_gain: float32 [6144], P('rep'), may hold values from 0.25 to 1.75
- expert_ids: int32 [1024, 2], P(('expert', 'hid')), may hold values from 0 to 3, as said below
- slot_ids: int32 [1024, 2], P(('expert', 'hid')), may hold values from 0 to 4, as said below
- w_gate: bfloat16 [4, 6144, 8192], P('expert', 'rep', 'hid'), may hold values from -0.078125 to 0.078125
- w_up: bfloat16 [4, 6144, 8192], P('expert', 'rep', 'hid'), may hold values from -0.078125 to 0.078125
- grad_gate: bfloat16 [4, 640, 8192], P('expert', None, 'hid'), may hold values from -1.1953125 to 1.1953125
- grad_up: bfloat16 [4, 640, 8192], P('expert', None, 'hid'), may hold values from -1.1953125 to 1.1953125
Outputs:
- grad_w_gate: bfloat16 [4, 6144, 8192], P('expert', 'rep', 'hid')
- grad_w_up: bfloat16 [4, 6144, 8192], P('expert', 'rep', 'hid')
- grad_tokens: bfloat16 [1024, 6144], P(('expert', 'hid'), 'rep')
Inputs may be any that keep to these rules, and one draw needn't show every extreme that they name: `expert_ids`: each token names two different experts; among the 8 tokens of one block, no expert is named more than 5 times and some expert exactly 5 times. Within one block of 8 tokens, the pairs (expert_ids[t, k], slot_ids[t, k]) are all different.
All inputs are finite; a program needn't handle non-finite values.
Results may differ from a plain program's by a relative error of at most 0.0049.
Values may be sent and summed in bfloat16 or wider, within the bound.
No kernel may reach another device: no remote copies, remote signals or barrier semaphores. Data moves between devices by JAX's collectives and lax.ppermute only.
A program may use at most 64 MiB of HBM per device.

v0:
```python
import jax
import jax.numpy as jnp
from jax import lax
from jax.sharding import Mesh
from jax.sharding import PartitionSpec as P


D = 6144
CAP = 5
TOK = 8
RING = ("zh", "zl")
LANES = 128


def exchange(x, axis):
    return lax.all_to_all(x, axis, 0, 0, tiled=True)


def copy_for_each(x, axis):
    size = lax.axis_size(axis)
    return exchange(jnp.broadcast_to(x[None], (size, *x.shape)), axis)


def feature_total(partial_value):
    return copy_for_each(partial_value[None], "rep").sum(axis=(0, 1))


def along(x, axis, step):
    size = lax.axis_size(axis)
    return lax.ppermute(x, axis, [(i, (i + step) % size) for i in range(size)])


def swap_cores(x):
    return lax.ppermute(x, "core", [(0, 1), (1, 0)])


def on_device(tokens, norm_gain, expert_ids, slot_ids, w_gate, w_up, grad_gate, grad_up):
    zh_n, core_n, x_n, zl_n = (lax.axis_size(a) for a in ("zh", "core", "x", "zl"))
    ring_n = zh_n * zl_n
    line_tokens = ring_n * TOK
    line_rows = zl_n * zh_n * core_n * CAP
    width = tokens.shape[1]
    core = lax.axis_index("core")
    mine = lax.axis_index("zh") * core_n + core
    partner = lax.axis_index("zh") * core_n + (1 - core)

    unit_contract = (((1,), (1,)), ((), ()))
    here = lax.axis_index("x")

    def part_for(step):
        at = lax.rem(here + step, x_n) * line_rows
        gate = lax.dynamic_slice_in_dim(grad_gate[0], at, line_rows)
        up = lax.dynamic_slice_in_dim(grad_up[0], at, line_rows)
        return lax.dot_general(
            gate, w_gate[0], unit_contract, preferred_element_type=jnp.float32
        ) + lax.dot_general(up, w_up[0], unit_contract, preferred_element_type=jnp.float32)

    arriving = []
    for step in (2, 1, 3):
        piece = part_for(step).astype(jnp.bfloat16)
        arriving.append(along(piece, "x", step).astype(jnp.float32))
    kept = part_for(0)

    code = (expert_ids * CAP + slot_ids).astype(jnp.bfloat16)
    tagged = jnp.concatenate([tokens, jnp.pad(code, ((0, 0), (0, LANES - 2)))], axis=1)
    line = copy_for_each(tagged, RING).reshape(line_tokens, width + LANES)
    line_values = line[:, :width]
    codes = line[:, width : width + 2].astype(jnp.int32)
    token = jnp.arange(line_tokens, dtype=jnp.int32)
    block = token // TOK
    base = (((block % zl_n) * zh_n + block // zl_n) * core_n + core) * CAP

    def rows_of(expert):
        slot = codes - expert * CAP
        return jnp.where((slot >= 0) & (slot < CAP), base[:, None] + slot, -1)

    row = jnp.arange(line_rows, dtype=jnp.int32)

    def choice(expert):
        at = rows_of(expert)
        return ((at[:, 0][:, None] == row[None]) | (at[:, 1][:, None] == row[None])).astype(
            jnp.bfloat16
        )

    to_mine = choice(mine)
    to_partner = choice(partner)
    first = (((0,), (0,)), ((), ()))

    def rows_from(chosen):
        return lax.dot_general(
            chosen, line_values, first, preferred_element_type=jnp.float32
        ).astype(jnp.bfloat16)

    own_rows = rows_from(to_mine) + swap_cores(rows_from(to_partner))
    steps = (0, 1, 3, 2)
    pieces = [own_rows]
    pieces += [along(own_rows, "x", step) for step in steps[1:]]

    values = tokens.astype(jnp.float32)
    squares = [jnp.sum(jnp.square(piece.astype(jnp.float32)), axis=1) for piece in pieces]
    squares += [jnp.sum(values * values, axis=1)]
    count = x_n * line_rows + TOK
    squares = jnp.pad(jnp.concatenate(squares), (0, -count % LANES)).reshape(-1, LANES)
    others = [along(squares, "rep", step) for step in (1, 3, 2)]
    squares = squares + others[0] + others[1] + others[2]
    rms = lax.rsqrt(squares / D + 1e-05).reshape(-1)[:count, None]
    row_rms, inverse_rms = rms[:-TOK], rms[-TOK:]
    scaled_in = values * inverse_rms
    raw = jnp.concatenate(pieces).astype(jnp.float32)
    gathered = (raw * row_rms * norm_gain).astype(jnp.bfloat16)

    def in_order(cotangent):
        return jnp.concatenate(
            [
                lax.dynamic_slice_in_dim(
                    cotangent, lax.rem(here - step + x_n, x_n) * line_rows, line_rows
                )
                for step in steps
            ]
        )

    new_gate = lax.dot_general(
        gathered, in_order(grad_gate[0]), first, preferred_element_type=jnp.float32
    )
    new_up = lax.dot_general(
        gathered, in_order(grad_up[0]), first, preferred_element_type=jnp.float32
    )

    line_sum = (kept + arriving[0] + arriving[1] + arriving[2]).astype(jnp.bfloat16)
    other_sum = swap_cores(line_sum)
    by_token = jnp.dot(to_mine, line_sum, preferred_element_type=jnp.float32) + jnp.dot(
        to_partner, other_sum, preferred_element_type=jnp.float32
    )
    by_token = by_token.astype(jnp.bfloat16).reshape(ring_n, TOK, width)
    normed_grad = exchange(by_token, RING).astype(jnp.float32).sum(axis=0)

    scaled = normed_grad * norm_gain
    dotted = feature_total(jnp.sum(scaled * scaled_in, axis=1)) / D
    grad_tokens = (inverse_rms * (scaled - scaled_in * dotted[:, None])).astype(jnp.bfloat16)
    return (new_gate.astype(jnp.bfloat16)[None], new_up.astype(jnp.bfloat16)[None], grad_tokens)


def solution(mesh):
    physical = Mesh(mesh.devices.reshape(2, 2, 4, 4, 8), ("zh", "core", "rep", "x", "zl"))
    expert, hid = ("zh", "core"), ("x", "zl")
    placed = (
        P(expert + hid, "rep"),
        P("rep"),
        P(expert + hid, None),
        P(expert + hid, None),
        P(expert, "rep", hid),
        P(expert, "rep", hid),
        P(expert, None, hid),
        P(expert, None, hid),
    )

    return jax.shard_map(
        on_device,
        mesh=physical,
        in_specs=placed,
        out_specs=(P(expert, "rep", hid), P(expert, "rep", hid), P(expert + hid, "rep")),
        check_vma=False,
    )
```

profile of v0, /device:TPU:6, one launch (start us, length us, event | category | flops | bytes accessed | tf_op | source)
XLA Modules:
  0.0 112.0 jit_solution(9222102058093833102)
XLA Ops:
  0.7 0.8 add_convert_fusion.1
  1.6 0.7 fusion.75
  2.3 0.8 broadcast_in_dim.13
  3.1 15.2 %all-to-all-start = ((bf16[16,8,1664]{2,1,0:T(8,128)(2,1)}), bf16[16,8,1664]{2,1,0:T(8,128)(2,1)S(1)}, u32[]{:S(2)}, u32[]{:S(2)}) async-start(bf16[16,8,1664]{2,1,0:T(8,128)(2,1)} %broadcast_in_dim.13), calls=%async_computation | async-start | bytes 851968 | tf_op jit(solution)/shard_map/all_to_all | solution.py:16
  18.4 0.7 dynamic-slice_bitcast_fusion.3
  19.1 0.4 fusion.18
  19.5 0.8 copy-done.1
  20.3 1.2 %fusion.2 = bf16[160,1536]{1,0:T(8,128)(2,1)} fusion(f32[160,1536]{1,0:T(8,128)S(1)} %fusion.18, bf16[160,256]{1,0:T(8,128)(2,1)S(1)} %get-tuple-element.12, bf16[1,1536,256]{2,1,0:T(8,128)(2,1)S(1)} %copy-done.1), kind=kOutput, calls=%fused_computation.10 | convolution fusion | flops 126320640 | bytes 2342912 | tf_op jit(solution)/shard_map/dot_general | solution.py:56
  21.5 3.3 %collective-permute-start.7 = (bf16[160,1536]{1,0:T(8,128)(2,1)}, bf16[160,1536]{1,0:T(8,128)(2,1)}, u32[]{:S(2)}, u32[]{:S(2)}) collective-permute-start(bf16[160,1536]{1,0:T(8,128)(2,1)} %fusion.2), channel_id=1, source_target_pairs={{0,16},{8,24},{16,0},{24,8},{1,17},{9,25},{17,1},{25,9},{2,18},{10... | collective-permute-start | bytes 1474568 | tf_op jit(solution)/shard_map/ppermute | solution.py:30
  24.9 0.4 fusion.16
  25.3 1.2 %fusion.3 = bf16[160,1536]{1,0:T(8,128)(2,1)} fusion(f32[160,1536]{1,0:T(8,128)S(1)} %fusion.16, bf16[160,256]{1,0:T(8,128)(2,1)S(1)} %get-tuple-element.10, bf16[1,1536,256]{2,1,0:T(8,128)(2,1)S(1)} %copy-done.1), kind=kOutput, calls=%fused_computation.11 | convolution fusion | flops 126320640 | bytes 2342912 | tf_op jit(solution)/shard_map/dot_general | solution.py:56
  26.5 4.0 %collective-permute-start.8 = (bf16[160,1536]{1,0:T(8,128)(2,1)}, bf16[160,1536]{1,0:T(8,128)(2,1)}, u32[]{:S(2)}, u32[]{:S(2)}) collective-permute-start(bf16[160,1536]{1,0:T(8,128)(2,1)} %fusion.3), channel_id=1, source_target_pairs={{0,8},{8,16},{16,24},{24,0},{1,9},{9,17},{17,25},{25,1},{2,10},{10... | collective-permute-start | bytes 1474568 | tf_op jit(solution)/shard_map/ppermute | solution.py:30
  30.5 0.4 fusion.14
  30.9 1.2 %fusion.4 = bf16[160,1536]{1,0:T(8,128)(2,1)} fusion(f32[160,1536]{1,0:T(8,128)S(1)} %fusion.14, bf16[160,256]{1,0:T(8,128)(2,1)S(1)} %get-tuple-element.11, bf16[1,1536,256]{2,1,0:T(8,128)(2,1)S(1)} %copy-done.1), kind=kOutput, calls=%fused_computation.12 | convolution fusion | flops 126320640 | bytes 2342912 | tf_op jit(solution)/shard_map/dot_general | solution.py:56
  32.1 1.9 %collective-permute-start.9 = (bf16[160,1536]{1,0:T(8,128)(2,1)}, bf16[160,1536]{1,0:T(8,128)(2,1)}, u32[]{:S(2)}, u32[]{:S(2)}) collective-permute-start(bf16[160,1536]{1,0:T(8,128)(2,1)} %fusion.4), channel_id=1, source_target_pairs={{0,24},{8,0},{16,8},{24,16},{1,25},{9,1},{17,9},{25,17},{2,26},{10... | collective-permute-start | bytes 1474568 | tf_op jit(solution)/shard_map/ppermute | solution.py:30
  34.0 0.5 add_multiply_fusion
  34.5 0.4 fusion.20
  34.9 8.5 %all-to-all-done = bf16[16,8,1664]{2,1,0:T(8,128)(2,1)S(1)} async-done(((bf16[16,8,1664]{2,1,0:T(8,128)(2,1)}), bf16[16,8,1664]{2,1,0:T(8,128)(2,1)S(1)}, u32[]{:S(2)}, u32[]{:S(2)}) %all-to-all-start) | async-done | bytes 426016 | tf_op jit(solution)/shard_map/all_to_all | solution.py:16
  43.5 0.7 fusion.56
  44.2 0.2 slice_reduce_fusion.1
  44.4 0.4 convolution_convert_fusion.2
  44.8 1.9 %collective-permute-start = (bf16[160,1536]{1,0:T(8,128)(2,1)S(1)}, bf16[160,1536]{1,0:T(8,128)(2,1)S(1)}, u32[]{:S(2)}, u32[]{:S(2)}) collective-permute-start(bf16[160,1536]{1,0:T(8,128)(2,1)S(1)} %convolution_convert_fusion.2), channel_id=1, source_target_pairs={{0,128},{128,0},{1,129},{129,1},{2,130},{130,2},{3,131},{131,3},{4... | collective-permute-start | bytes 1474568 | tf_op jit(solution)/shard_map/ppermute | solution.py:34
  46.8 2.0 %collective-permute-done.9 = bf16[160,1536]{1,0:T(8,128)(2,1)} collective-permute-done((bf16[160,1536]{1,0:T(8,128)(2,1)}, bf16[160,1536]{1,0:T(8,128)(2,1)}, u32[]{:S(2)}, u32[]{:S(2)}) %collective-permute-start.9) | collective-permute-done | bytes 491552 | tf_op jit(solution)/shard_map/ppermute | solution.py:30
  48.7 1.8 %add_convert_fusion = bf16[160,1536]{1,0:T(8,128)(2,1)S(1)} fusion(bf16[160,1536]{1,0:T(8,128)(2,1)} %collective-permute-done.9, bf16[160,1536]{1,0:T(8,128)(2,1)} %collective-permute-done.8, bf16[160,1536]{1,0:T(8,128)(2,1)} %collective-permute-done.7, f32[160,1536]{1,0:T(8,128)S(1)} %fusion.20, bf16[1,1536,256]{2,1,0:T(8,128)(2,1)S(1)} %copy-done.1, ...), kind=kOutput, calls=%fused_computation.18 | convolution fusion | flops 127795200 | bytes 3817476 | tf_op jit(solution)/shard_map/dot_general | solution.py:56
  50.6 1.9 %collective-permute-start.10 = (bf16[160,1536]{1,0:T(8,128)(2,1)S(1)}, bf16[160,1536]{1,0:T(8,128)(2,1)S(1)}, u32[]{:S(2)}, u32[]{:S(2)}) collective-permute-start(bf16[160,1536]{1,0:T(8,128)(2,1)S(1)} %add_convert_fusion), channel_id=1, source_target_pairs={{0,128},{128,0},{1,129},{129,1},{2,130},{130,2},{3,131},{131,3},{4... | collective-permute-start | bytes 1474568 | tf_op jit(solution)/shard_map/ppermute | solution.py:34
  52.7 1.2 %multiply_reduce_fusion.3 = (f32[160]{0:T(256)S(1)}, bf16[160,1536]{1,0:T(8,128)(2,1)}) fusion(bf16[160,1536]{1,0:T(8,128)(2,1)S(1)} %collective-permute-done, bf16[128,1664]{1,0:T(8,128)(2,1)S(1)} %bitcast.67, s32[128]{0:T(128)S(1)} %get-tuple-element.4, s32[128]{0:T(128)S(1)} %get-tuple-element.3), kind=kOutput, calls=%fused_computation.22 | convolution fusion | flops 64204640 | bytes 1377920 | tf_op jit(solution)/shard_map/dot_general | solution.py:90
  53.9 3.1 %collective-permute-start.3 = (bf16[160,1536]{1,0:T(8,128)(2,1)}, bf16[160,1536]{1,0:T(8,128)(2,1)S(1)}, u32[]{:S(2)}, u32[]{:S(2)}) collective-permute-start(bf16[160,1536]{1,0:T(8,128)(2,1)} %get-tuple-element.18), channel_id=1, source_target_pairs={{0,16},{8,24},{16,0},{24,8},{1,17},{9,25},{17,1},{25,9},{2,18},{10... | collective-permute-start | bytes 1474568 | tf_op jit(solution)/shard_map/ppermute | solution.py:30
  57.0 1.9 %collective-permute-start.2 = (bf16[160,1536]{1,0:T(8,128)(2,1)}, bf16[160,1536]{1,0:T(8,128)(2,1)S(1)}, u32[]{:S(2)}, u32[]{:S(2)}) collective-permute-start(bf16[160,1536]{1,0:T(8,128)(2,1)} %get-tuple-element.18), channel_id=1, source_target_pairs={{0,24},{8,0},{16,8},{24,16},{1,25},{9,1},{17,9},{25,17},{2,26},{10... | collective-permute-start | bytes 1474568 | tf_op jit(solution)/shard_map/ppermute | solution.py:30
  59.0 0.3 fusion.40
  59.3 5.1 %collective-permute-start.1 = (bf16[160,1536]{1,0:T(8,128)(2,1)}, bf16[160,1536]{1,0:T(8,128)(2,1)S(1)}, u32[]{:S(2)}, u32[]{:S(2)}) collective-permute-start(bf16[160,1536]{1,0:T(8,128)(2,1)} %get-tuple-element.18), channel_id=1, source_target_pairs={{0,8},{8,16},{16,24},{24,0},{1,9},{9,17},{17,25},{25,1},{2,10},{10... | collective-permute-start | bytes 1474568 | tf_op jit(solution)/shard_map/ppermute | solution.py:30
  64.4 1.1 fusion.7
  65.5 11.9 %all-to-all-start.1 = ((bf16[16,8,1536]{2,1,0:T(8,128)(2,1)}), bf16[16,8,1536]{2,1,0:T(8,128)(2,1)S(1)}, u32[]{:S(2)}, u32[]{:S(2)}) async-start(bf16[16,8,1536]{2,1,0:T(8,128)(2,1)} %fusion.7), calls=%async_computation.1 | async-start | bytes 786432 | tf_op jit(solution)/shard_map/all_to_all | solution.py:16
  77.5 0.2 multiply_reduce_fusion
  77.7 4.0 %collective-permute-done.2 = bf16[160,1536]{1,0:T(8,128)(2,1)S(1)} collective-permute-done((bf16[160,1536]{1,0:T(8,128)(2,1)}, bf16[160,1536]{1,0:T(8,128)(2,1)S(1)}, u32[]{:S(2)}, u32[]{:S(2)}) %collective-permute-start.2) | collective-permute-done | bytes 491552 | tf_op jit(solution)/shard_map/ppermute | solution.py:30
  81.7 0.2 multiply_reduce_fusion.1
  81.8 0.2 multiply_reduce_fusion.2
  82.1 3.5 %collective-permute-start.4 = (f32[6,128]{1,0:T(8,128)S(1)}, f32[6,128]{1,0:T(8,128)S(1)}, u32[]{:S(2)}, u32[]{:S(2)}) collective-permute-start(f32[6,128]{1,0:T(8,128)S(1)} %pad_bitcast_fusion), channel_id=1, source_target_pairs={{0,32},{32,64},{64,96},{96,0},{1,33},{33,65},{65,97},{97,1},{2,34}... | collective-permute-start | bytes 9224 | tf_op jit(solution)/shard_map/ppermute | solution.py:30
  85.6 3.6 %collective-permute-start.5 = (f32[6,128]{1,0:T(8,128)S(1)}, f32[6,128]{1,0:T(8,128)S(1)}, u32[]{:S(2)}, u32[]{:S(2)}) collective-permute-start(f32[6,128]{1,0:T(8,128)S(1)} %pad_bitcast_fusion), channel_id=1, source_target_pairs={{0,96},{32,0},{64,32},{96,64},{1,97},{33,1},{65,33},{97,65},{2,98}... | collective-permute-start | bytes 9224 | tf_op jit(solution)/shard_map/ppermute | solution.py:30
  89.2 3.9 %collective-permute-start.6 = (f32[6,128]{1,0:T(8,128)S(1)}, f32[6,128]{1,0:T(8,128)S(1)}, u32[]{:S(2)}, u32[]{:S(2)}) collective-permute-start(f32[6,128]{1,0:T(8,128)S(1)} %pad_bitcast_fusion), channel_id=1, source_target_pairs={{0,64},{32,96},{64,0},{96,32},{1,65},{33,97},{65,1},{97,33},{2,66}... | collective-permute-start | bytes 9224 | tf_op jit(solution)/shard_map/ppermute | solution.py:30
  93.1 3.1 %collective-permute-done.6 = f32[6,128]{1,0:T(8,128)S(1)} collective-permute-done((f32[6,128]{1,0:T(8,128)S(1)}, f32[6,128]{1,0:T(8,128)S(1)}, u32[]{:S(2)}, u32[]{:S(2)}) %collective-permute-start.6) | collective-permute-done | bytes 3104 | tf_op jit(solution)/shard_map/ppermute | solution.py:30
  96.3 3.0 %fusion.1 = bf16[1,1536,256]{2,1,0:T(8,128)(2,1)} fusion(bf16[160,256]{1,0:T(8,128)(2,1)S(1)} %copy-done.10, bf16[160,256]{1,0:T(8,128)(2,1)S(1)} %copy-done.6, bf16[160,256]{1,0:T(8,128)(2,1)S(1)} %copy-done.8, bf16[160,256]{1,0:T(8,128)(2,1)S(1)} %copy-done.12, bf16[160,1536]{1,0:T(8,128)(2,1)S(1)} %collective-permute-done.3, ...), kind=kOutput, calls=%fused_computation.9 | convolution fusion | flops 515833856 | bytes 3088896 | tf_op jit(solution)/shard_map/dot_general | solution.py:125
  99.2 1.6 %all-to-all-done.1 = bf16[16,8,1536]{2,1,0:T(8,128)(2,1)S(1)} async-done(((bf16[16,8,1536]{2,1,0:T(8,128)(2,1)}), bf16[16,8,1536]{2,1,0:T(8,128)(2,1)S(1)}, u32[]{:S(2)}, u32[]{:S(2)}) %all-to-all-start.1) | async-done | bytes 393248 | tf_op jit(solution)/shard_map/all_to_all | solution.py:16
  100.9 0.2 fusion.70
  101.1 0.6 broadcast_in_dim.17
  101.7 4.5 %all-to-all-start.2 = ((f32[4,1,8]{2,1,0:T(1,128)}), f32[4,1,8]{2,1,0:T(1,128)S(1)}, u32[]{:S(2)}, u32[]{:S(2)}) async-start(f32[4,1,8]{2,1,0:T(1,128)} %broadcast_in_dim.17), calls=%async_computation.2 | async-start | bytes 4096 | tf_op jit(solution)/shard_map/all_to_all | solution.py:16
  106.1 2.9 %fusion = bf16[1,1536,256]{2,1,0:T(8,128)(2,1)} fusion(bf16[160,256]{1,0:T(8,128)(2,1)S(1)} %get-tuple-element.19, bf16[160,256]{1,0:T(8,128)(2,1)S(1)} %get-tuple-element.21, bf16[160,256]{1,0:T(8,128)(2,1)S(1)} %get-tuple-element.20, bf16[160,256]{1,0:T(8,128)(2,1)S(1)} %copy-done.11, bf16[160,1536]{1,0:T(8,128)(2,1)S(1)} %collective-permute-done.3, ...), kind=kOutput, calls=%fused_computation.8 | convolution fusion | flops 515833856 | bytes 3088896 | tf_op jit(solution)/shard_map/dot_general | solution.py:122
  109.0 2.3 %all-to-all-done.2 = f32[4,1,8]{2,1,0:T(1,128)S(1)} async-done(((f32[4,1,8]{2,1,0:T(1,128)}), f32[4,1,8]{2,1,0:T(1,128)S(1)}, u32[]{:S(2)}, u32[]{:S(2)}) %all-to-all-start.2) | async-done | bytes 160 | tf_op jit(solution)/shard_map/all_to_all | solution.py:16
  111.4 0.7 fusion.73
  (46 shorter events, 0.7 us)
Async XLA Ops:
  0.6 18.5 %copy-start = (bf16[1,1536,256]{2,1,0:T(8,128)(2,1)S(1)}, bf16[1,1536,256]{2,1,0:T(8,128)(2,1)}, u32[]{:S(2)}) copy-start(bf16[1,1536,256]{2,1,0:T(8,128)(2,1)} %param.12) | copy-start | bytes 2359300
  0.6 17.7 %copy-start.2 = (bf16[1,640,256]{2,1,0:T(8,128)(2,1)S(1)}, bf16[1,640,256]{2,1,0:T(8,128)(2,1)}, u32[]{:S(2)}) copy-start(bf16[1,640,256]{2,1,0:T(8,128)(2,1)} %param.14) | copy-start | bytes 983044
  0.7 17.7 %copy-start.3 = (bf16[1,640,256]{2,1,0:T(8,128)(2,1)S(1)}, bf16[1,640,256]{2,1,0:T(8,128)(2,1)}, u32[]{:S(2)}) copy-start(bf16[1,640,256]{2,1,0:T(8,128)(2,1)} %param.15) | copy-start | bytes 983044
  3.1 40.3 %all-to-all-start = ((bf16[16,8,1664]{2,1,0:T(8,128)(2,1)}), bf16[16,8,1664]{2,1,0:T(8,128)(2,1)S(1)}, u32[]{:S(2)}, u32[]{:S(2)}) async-start(bf16[16,8,1664]{2,1,0:T(8,128)(2,1)} %broadcast_in_dim.13), calls=%async_computation | async-start | bytes 851968 | tf_op jit(solution)/shard_map/all_to_all | solution.py:16
  19.1 2.4 %copy-start.9 = (bf16[160,256]{1,0:T(8,128)(2,1)}, bf16[160,256]{1,0:T(8,128)(2,1)S(1)}, u32[]{:S(2)}) copy-start(bf16[160,256]{1,0:T(8,128)(2,1)S(1)} %get-tuple-element.12) | copy-start | bytes 245764
  19.1 6.2 %copy-start.5 = (bf16[160,256]{1,0:T(8,128)(2,1)}, bf16[160,256]{1,0:T(8,128)(2,1)S(1)}, u32[]{:S(2)}) copy-start(bf16[160,256]{1,0:T(8,128)(2,1)S(1)} %get-tuple-element.10) | copy-start | bytes 245764
  19.1 11.8 %copy-start.7 = (bf16[160,256]{1,0:T(8,128)(2,1)}, bf16[160,256]{1,0:T(8,128)(2,1)S(1)}, u32[]{:S(2)}) copy-start(bf16[160,256]{1,0:T(8,128)(2,1)S(1)} %get-tuple-element.11) | copy-start | bytes 245764
  19.1 1.2 %copy-start.1 = (bf16[1,1536,256]{2,1,0:T(8,128)(2,1)S(1)}, bf16[1,1536,256]{2,1,0:T(8,128)(2,1)}, u32[]{:S(2)}) copy-start(bf16[1,1536,256]{2,1,0:T(8,128)(2,1)} %param.13) | copy-start | bytes 2359300
  21.5 25.2 %collective-permute-start.7 = (bf16[160,1536]{1,0:T(8,128)(2,1)}, bf16[160,1536]{1,0:T(8,128)(2,1)}, u32[]{:S(2)}, u32[]{:S(2)}) collective-permute-start(bf16[160,1536]{1,0:T(8,128)(2,1)} %fusion.2), channel_id=1, source_target_pairs={{0,16},{8,24},{16,0},{24,8},{1,17},{9,25},{17,1},{25,9},{2,18},{10... | collective-permute-start | bytes 1474568 | tf_op jit(solution)/shard_map/ppermute | solution.py:30
  26.5 20.3 %collective-permute-start.8 = (bf16[160,1536]{1,0:T(8,128)(2,1)}, bf16[160,1536]{1,0:T(8,128)(2,1)}, u32[]{:S(2)}, u32[]{:S(2)}) collective-permute-start(bf16[160,1536]{1,0:T(8,128)(2,1)} %fusion.3), channel_id=1, source_target_pairs={{0,8},{8,16},{16,24},{24,0},{1,9},{9,17},{17,25},{25,1},{2,10},{10... | collective-permute-start | bytes 1474568 | tf_op jit(solution)/shard_map/ppermute | solution.py:30
  32.1 16.7 %collective-permute-start.9 = (bf16[160,1536]{1,0:T(8,128)(2,1)}, bf16[160,1536]{1,0:T(8,128)(2,1)}, u32[]{:S(2)}, u32[]{:S(2)}) collective-permute-start(bf16[160,1536]{1,0:T(8,128)(2,1)} %fusion.4), channel_id=1, source_target_pairs={{0,24},{8,0},{16,8},{24,16},{1,25},{9,1},{17,9},{25,17},{2,26},{10... | collective-permute-start | bytes 1474568 | tf_op jit(solution)/shard_map/ppermute | solution.py:30
  44.8 7.9 %collective-permute-start = (bf16[160,1536]{1,0:T(8,128)(2,1)S(1)}, bf16[160,1536]{1,0:T(8,128)(2,1)S(1)}, u32[]{:S(2)}, u32[]{:S(2)}) collective-permute-start(bf16[160,1536]{1,0:T(8,128)(2,1)S(1)} %convolution_convert_fusion.2), channel_id=1, source_target_pairs={{0,128},{128,0},{1,129},{129,1},{2,130},{130,2},{3,131},{131,3},{4... | collective-permute-start | bytes 1474568 | tf_op jit(solution)/shard_map/ppermute | solution.py:34
  50.6 8.4 %collective-permute-start.10 = (bf16[160,1536]{1,0:T(8,128)(2,1)S(1)}, bf16[160,1536]{1,0:T(8,128)(2,1)S(1)}, u32[]{:S(2)}, u32[]{:S(2)}) collective-permute-start(bf16[160,1536]{1,0:T(8,128)(2,1)S(1)} %add_convert_fusion), channel_id=1, source_target_pairs={{0,128},{128,0},{1,129},{129,1},{2,130},{130,2},{3,131},{131,3},{4... | collective-permute-start | bytes 1474568 | tf_op jit(solution)/shard_map/ppermute | solution.py:34
  53.9 23.6 %collective-permute-start.3 = (bf16[160,1536]{1,0:T(8,128)(2,1)}, bf16[160,1536]{1,0:T(8,128)(2,1)S(1)}, u32[]{:S(2)}, u32[]{:S(2)}) collective-permute-start(bf16[160,1536]{1,0:T(8,128)(2,1)} %get-tuple-element.18), channel_id=1, source_target_pairs={{0,16},{8,24},{16,0},{24,8},{1,17},{9,25},{17,1},{25,9},{2,18},{10... | collective-permute-start | bytes 1474568 | tf_op jit(solution)/shard_map/ppermute | solution.py:30
  57.0 24.6 %collective-permute-start.2 = (bf16[160,1536]{1,0:T(8,128)(2,1)}, bf16[160,1536]{1,0:T(8,128)(2,1)S(1)}, u32[]{:S(2)}, u32[]{:S(2)}) collective-permute-start(bf16[160,1536]{1,0:T(8,128)(2,1)} %get-tuple-element.18), channel_id=1, source_target_pairs={{0,24},{8,0},{16,8},{24,16},{1,25},{9,1},{17,9},{25,17},{2,26},{10... | collective-permute-start | bytes 1474568 | tf_op jit(solution)/shard_map/ppermute | solution.py:30
  59.3 18.1 %copy-start.4 = (bf16[8,1536]{1,0:T(8,128)(2,1)S(1)}, bf16[8,1536]{1,0:T(8,128)(2,1)}, u32[]{:S(2)}) copy-start(bf16[8,1536]{1,0:T(8,128)(2,1)} %param.8) | copy-start | bytes 73732
  59.3 22.6 %collective-permute-start.1 = (bf16[160,1536]{1,0:T(8,128)(2,1)}, bf16[160,1536]{1,0:T(8,128)(2,1)S(1)}, u32[]{:S(2)}, u32[]{:S(2)}) collective-permute-start(bf16[160,1536]{1,0:T(8,128)(2,1)} %get-tuple-element.18), channel_id=1, source_target_pairs={{0,8},{8,16},{16,24},{24,0},{1,9},{9,17},{17,25},{25,1},{2,10},{10... | collective-permute-start | bytes 1474568 | tf_op jit(solution)/shard_map/ppermute | solution.py:30
  65.5 30.7 %copy-start.6 = (bf16[160,256]{1,0:T(8,128)(2,1)S(1)}, bf16[160,256]{1,0:T(8,128)(2,1)}, u32[]{:S(2)}) copy-start(bf16[160,256]{1,0:T(8,128)(2,1)} %copy-done.5) | copy-start | bytes 245764
  65.5 30.7 %copy-start.8 = (bf16[160,256]{1,0:T(8,128)(2,1)S(1)}, bf16[160,256]{1,0:T(8,128)(2,1)}, u32[]{:S(2)}) copy-start(bf16[160,256]{1,0:T(8,128)(2,1)} %copy-done.7) | copy-start | bytes 245764
  65.5 30.7 %copy-start.10 = (bf16[160,256]{1,0:T(8,128)(2,1)S(1)}, bf16[160,256]{1,0:T(8,128)(2,1)}, u32[]{:S(2)}) copy-start(bf16[160,256]{1,0:T(8,128)(2,1)} %copy-done.9) | copy-start | bytes 245764
  65.5 30.8 %copy-start.12 = (bf16[160,256]{1,0:T(8,128)(2,1)S(1)}, bf16[160,256]{1,0:T(8,128)(2,1)}, u32[]{:S(2)}) copy-start(bf16[160,256]{1,0:T(8,128)(2,1)} %get-tuple-element.9) | copy-start | bytes 245764
  65.5 30.8 %copy-start.13 = (f32[1536]{0:T(1024)S(1)}, f32[1536]{0:T(1024)}, u32[]{:S(2)}) copy-start(f32[1536]{0:T(1024)} %param.9) | copy-start | bytes 18436
  65.5 35.3 %all-to-all-start.1 = ((bf16[16,8,1536]{2,1,0:T(8,128)(2,1)}), bf16[16,8,1536]{2,1,0:T(8,128)(2,1)S(1)}, u32[]{:S(2)}, u32[]{:S(2)}) async-start(bf16[16,8,1536]{2,1,0:T(8,128)(2,1)} %fusion.7), calls=%async_computation.1 | async-start | bytes 786432 | tf_op jit(solution)/shard_map/all_to_all | solution.py:16
  82.1 11.0 %collective-permute-start.4 = (f32[6,128]{1,0:T(8,128)S(1)}, f32[6,128]{1,0:T(8,128)S(1)}, u32[]{:S(2)}, u32[]{:S(2)}) collective-permute-start(f32[6,128]{1,0:T(8,128)S(1)} %pad_bitcast_fusion), channel_id=1, source_target_pairs={{0,32},{32,64},{64,96},{96,0},{1,33},{33,65},{65,97},{97,1},{2,34}... | collective-permute-start | bytes 9224 | tf_op jit(solution)/shard_map/ppermute | solution.py:30
  85.6 7.5 %collective-permute-start.5 = (f32[6,128]{1,0:T(8,128)S(1)}, f32[6,128]{1,0:T(8,128)S(1)}, u32[]{:S(2)}, u32[]{:S(2)}) collective-permute-start(f32[6,128]{1,0:T(8,128)S(1)} %pad_bitcast_fusion), channel_id=1, source_target_pairs={{0,96},{32,0},{64,32},{96,64},{1,97},{33,1},{65,33},{97,65},{2,98}... | collective-permute-start | bytes 9224 | tf_op jit(solution)/shard_map/ppermute | solution.py:30
  89.2 7.0 %collective-permute-start.6 = (f32[6,128]{1,0:T(8,128)S(1)}, f32[6,128]{1,0:T(8,128)S(1)}, u32[]{:S(2)}, u32[]{:S(2)}) collective-permute-start(f32[6,128]{1,0:T(8,128)S(1)} %pad_bitcast_fusion), channel_id=1, source_target_pairs={{0,64},{32,96},{64,0},{96,32},{1,65},{33,97},{65,1},{97,33},{2,66}... | collective-permute-start | bytes 9224 | tf_op jit(solution)/shard_map/ppermute | solution.py:30
  96.3 9.8 %copy-start.11 = (bf16[160,256]{1,0:T(8,128)(2,1)S(1)}, bf16[160,256]{1,0:T(8,128)(2,1)}, u32[]{:S(2)}) copy-start(bf16[160,256]{1,0:T(8,128)(2,1)} %get-tuple-element.22) | copy-start | bytes 245764
  101.7 9.7 %all-to-all-start.2 = ((f32[4,1,8]{2,1,0:T(1,128)}), f32[4,1,8]{2,1,0:T(1,128)S(1)}, u32[]{:S(2)}, u32[]{:S(2)}) async-start(f32[4,1,8]{2,1,0:T(1,128)} %broadcast_in_dim.17), calls=%async_computation.2 | async-start | bytes 4096 | tf_op jit(solution)/shard_map/all_to_all | solution.py:16
where the time goes:
time: 113 us; the launch traced here: 112 us
  starting transfers between devices  65.6 us (58%)
  waiting for transfers between devices  21.5 us (19%)
  matrix products  15.9 us (14%)
  other arithmetic  4.46 us (4%)
  local copies, waits for them, and re-layouts  3.52 us (3%)
    all_to_all x3, starting transfers between devices, exchange(): return lax.all_to_all(x, axis, 0, 0, tiled=True)  31.5 us
    ppermute x9, starting transfers between devices, along(): return lax.ppermute(x, axis, [(i, (i + step) % size) for i in range(size)])  30.3 us
    all_to_all x3, waiting for transfers between devices, exchange(): return lax.all_to_all(x, axis, 0, 0, tiled=True)  12.4 us
    ppermute x9, waiting for transfers between devices, along(): return lax.ppermute(x, axis, [(i, (i + step) % size) for i in range(size)])  9.05 us
    dot_general x4, matrix products, part_for(): lax.dot_general(up, w_up[0], unit_contract, preferred_element_type=jnp.fl...  5.44 us
    ppermute x2, starting transfers between devices, swap_cores(): return lax.ppermute(x, 'core', [(0, 1), (1, 0)])  3.84 us
    dot_general x1, matrix products, on_device(): lax.dot_general(gathered, in_order(grad_up[0]), first, preferred_element_...  2.96 us
    dot_general x1, matrix products, on_device(): lax.dot_general(gathered, in_order(grad_gate[0]), first, preferred_elemen...  2.92 us
  transfers between devices with their start and end apart: 14, of which 6 were waited for; matrix products, arithmetic and copies ran while one was open for 17% of the time, Pallas kernels for 0%

commit v1 on v0

--- a/solution.py
+++ b/solution.py
@@ -59,7 +59,6 @@
     for step in (2, 1, 3):
         piece = part_for(step).astype(jnp.bfloat16)
         arriving.append(along(piece, "x", step).astype(jnp.float32))
-    kept = part_for(0)
 
     code = (expert_ids * CAP + slot_ids).astype(jnp.bfloat16)
     tagged = jnp.concatenate([tokens, jnp.pad(code, ((0, 0), (0, LANES - 2)))], axis=1)
@@ -91,21 +90,35 @@
             chosen, line_values, first, preferred_element_type=jnp.float32
         ).astype(jnp.bfloat16)
 
-    own_rows = rows_from(to_mine) + swap_cores(rows_from(to_partner))
+    for_partner = rows_from(to_partner)
+    from_partner = swap_cores(for_partner)
+    own_rows = rows_from(to_mine) + from_partner
     steps = (0, 1, 3, 2)
     pieces = [own_rows]
     pieces += [along(own_rows, "x", step) for step in steps[1:]]
 
+    line_sum = (part_for(0) + arriving[0] + arriving[1] + arriving[2]).astype(jnp.bfloat16)
+    other_sum = swap_cores(line_sum)
+    by_token = jnp.dot(to_mine, line_sum, preferred_element_type=jnp.float32) + jnp.dot(
+        to_partner, other_sum, preferred_element_type=jnp.float32
+    )
+    by_token = by_token.astype(jnp.bfloat16).reshape(ring_n, TOK, width)
+    normed_grad = exchange(by_token, RING).astype(jnp.float32).sum(axis=0)
+
+    scaled = normed_grad * norm_gain
+
     values = tokens.astype(jnp.float32)
-    squares = [jnp.sum(jnp.square(piece.astype(jnp.float32)), axis=1) for piece in pieces]
-    squares += [jnp.sum(values * values, axis=1)]
-    count = x_n * line_rows + TOK
-    squares = jnp.pad(jnp.concatenate(squares), (0, -count % LANES)).reshape(-1, LANES)
-    others = [along(squares, "rep", step) for step in (1, 3, 2)]
-    squares = squares + others[0] + others[1] + others[2]
-    rms = lax.rsqrt(squares / D + 1e-05).reshape(-1)[:count, None]
-    row_rms, inverse_rms = rms[:-TOK], rms[-TOK:]
-    scaled_in = values * inverse_rms
+    totals = [jnp.sum(jnp.square(piece.astype(jnp.float32)), axis=1) for piece in pieces]
+    totals += [jnp.sum(values * values, axis=1), jnp.sum(scaled * values, axis=1)]
+    rows_n = x_n * line_rows
+    count = rows_n + 2 * TOK
+    totals = jnp.pad(jnp.concatenate(totals), (0, -count % LANES))
+    totals = feature_total(totals)
+    rms = lax.rsqrt(totals[: rows_n + TOK] / D + 1e-05)[:, None]
+    row_rms, inverse_rms = rms[:rows_n], rms[rows_n:]
+    dotted = inverse_rms * totals[rows_n + TOK : count, None] / D
+    grad_tokens = (inverse_rms * (scaled - values * inverse_rms * dotted)).astype(jnp.bfloat16)
+
     raw = jnp.concatenate(pieces).astype(jnp.float32)
     gathered = (raw * row_rms * norm_gain).astype(jnp.bfloat16)
 
@@ -126,17 +139,6 @@
         gathered, in_order(grad_up[0]), first, preferred_element_type=jnp.float32
     )
 
-    line_sum = (kept + arriving[0] + arriving[1] + arriving[2]).astype(jnp.bfloat16)
-    other_sum = swap_cores(line_sum)
-    by_token = jnp.dot(to_mine, line_sum, preferred_element_type=jnp.float32) + jnp.dot(
-        to_partner, other_sum, preferred_element_type=jnp.float32
-    )
-    by_token = by_token.astype(jnp.bfloat16).reshape(ring_n, TOK, width)
-    normed_grad = exchange(by_token, RING).astype(jnp.float32).sum(axis=0)
-
-    scaled = normed_grad * norm_gain
-    dotted = feature_total(jnp.sum(scaled * scaled_in, axis=1)) / D
-    grad_tokens = (inverse_rms * (scaled - scaled_in * dotted[:, None])).astype(jnp.bfloat16)
     return (new_gate.astype(jnp.bfloat16)[None], new_up.astype(jnp.bfloat16)[None], grad_tokens)
 
 

time: 113 us -> 113 us (level)
  starting transfers between devices: 65.6 us -> 49.7 us
  blocking collectives: 0 us -> 9.61 us
  waiting for transfers between devices: 21.5 us -> 29.4 us
  other arithmetic: 4.46 us -> 2.84 us
    ppermute x9 -> x6, waiting for transfers between devices: 9.05 us -> 29.4 us  [along(): return lax.ppermute(x, axis, [(i, (i + step) % size) for i in range(size)])]
    all_to_all x3 -> x2, waiting for transfers between devices: 12.4 us -> 0.01 us  [exchange(): return lax.all_to_all(x, axis, 0, 0, tiled=True)]
    ppermute x9 -> x6, starting transfers between devices: 30.3 us -> 18.4 us  [along(): return lax.ppermute(x, axis, [(i, (i + step) % size) for i in range(size)])]
    all_to_all x0 -> x1, blocking collectives: none -> 9.61 us  [exchange(): return lax.all_to_all(x, axis, 0, 0, tiled=True)]
    all_to_all x3 -> x2, starting transfers between devices: 31.5 us -> 26.9 us  [exchange(): return lax.all_to_all(x, axis, 0, 0, tiled=True)]
    dynamic_slice x1, local copies, waits for them, and re-layouts: 0.71 us -> 1.95 us  [in_order(): lax.dynamic_slice_in_dim(cotangent, lax.rem(here - step + x_n, x_n) * lin...]
  transfers between devices with their start and end apart: 14 -> 10, of which waited for: 6 -> 4; matrix products, arithmetic and copies ran while one was open for 17% -> 11% of each run, Pallas kernels for 0% -> 0%
where the time goes in v1:
time: 113 us; the launch traced here: 112 us
  starting transfers between devices  49.7 us (44%)
  waiting for transfers between devices  29.4 us (26%)
  matrix products  15.2 us (13%)
  blocking collectives  9.61 us (9%)
  local copies, waits for them, and re-layouts  4.19 us (4%)
  other arithmetic  2.84 us (3%)
    ppermute x6, waiting for transfers between devices, along(): return lax.ppermute(x, axis, [(i, (i + step) % size) for i in range(size)])  29.4 us
    all_to_all x2, starting transfers between devices, exchange(): return lax.all_to_all(x, axis, 0, 0, tiled=True)  26.9 us
    ppermute x6, starting transfers between devices, along(): return lax.ppermute(x, axis, [(i, (i + step) % size) for i in range(size)])  18.4 us
    all_to_all x1, blocking collectives, exchange(): return lax.all_to_all(x, axis, 0, 0, tiled=True)  9.61 us
    dot_general x4, matrix products, part_for(): lax.dot_general(up, w_up[0], unit_contract, preferred_element_type=jnp.fl...  4.36 us
    ppermute x2, starting transfers between devices, swap_cores(): return lax.ppermute(x, 'core', [(0, 1), (1, 0)])  4.33 us
    dot_general x1, matrix products, on_device(): lax.dot_general(gathered, in_order(grad_up[0]), first, preferred_element_...  3.06 us
    dot_general x4, matrix products, part_for(): lax.dot_general(gate, w_gate[0], unit_contract, preferred_element_type=jn...  2.51 us
  transfers between devices with their start and end apart: 10, of which 4 were waited for; matrix products, arithmetic and copies ran while one was open for 11% of the time, Pallas kernels for 0%

profile of v1, /device:TPU:6, one launch (start us, length us, event | category | flops | bytes accessed | tf_op | source)
XLA Modules:
  0.0 112.1 jit_solution(5995121494314323215)
XLA Ops:
  0.6 0.0 copy-start
  0.7 1.9 %dynamic-slice_bitcast_fusion = (bf16[160,256]{1,0:T(8,128)(2,1)}, bf16[160,256]{1,0:T(8,128)(2,1)S(1)}, bf16[160,256]{1,0:T(8,128)(2,1)S(1)}, bf16[160,256]{1,0...) fusion(bf16[1,640,256]{2,1,0:T(8,128)(2,1)} %param.15, ...), kind=kLoop, calls=%fused_computation.69 | loop fusion | bytes 1310736 | tf_op jit(solution)/shard_map/dynamic_slice | solution.py:128
  2.7 0.4 fusion.18
  3.1 0.2 copy-done.2
  3.3 0.6 copy-done.1
  3.9 0.4 fusion.2
  4.3 3.3 %collective-permute-start.4 = (bf16[160,1536]{1,0:T(8,128)(2,1)S(1)}, bf16[160,1536]{1,0:T(8,128)(2,1)S(1)}, u32[]{:S(2)}, u32[]{:S(2)}) collective-permute-start(bf16[160,1536]{1,0:T(8,128)(2,1)S(1)} %fusion.2), channel_id=1, source_target_pairs={{0,16},{8,24},{16,0},{24,8},{1,17},{9,25},{17,1},{25,9},{2,18},{10... | collective-permute-start | bytes 1474568 | tf_op jit(solution)/shard_map/ppermute | solution.py:30
  7.7 0.1 copy.21
  7.8 0.8 broadcast_in_dim.13
  8.6 15.2 %all-to-all-start = ((bf16[16,8,1664]{2,1,0:T(8,128)(2,1)}), bf16[16,8,1664]{2,1,0:T(8,128)(2,1)S(1)}, u32[]{:S(2)}, u32[]{:S(2)}) async-start(bf16[16,8,1664]{2,1,0:T(8,128)(2,1)} %broadcast_in_dim.13), calls=%async_computation | async-start | bytes 851968 | tf_op jit(solution)/shard_map/all_to_all | solution.py:16
  23.8 0.4 fusion.16
  24.2 1.2 %fusion.3 = bf16[160,1536]{1,0:T(8,128)(2,1)} fusion(f32[160,1536]{1,0:T(8,128)S(1)} %fusion.16, bf16[160,256]{1,0:T(8,128)(2,1)S(1)} %get-tuple-element.12, bf16[1,1536,256]{2,1,0:T(8,128)(2,1)S(1)} %copy-done.1), kind=kOutput, calls=%fused_computation.11 | convolution fusion | flops 126320640 | bytes 2342912 | tf_op jit(solution)/shard_map/dot_general | solution.py:56
  25.4 4.1 %collective-permute-start.5 = (bf16[160,1536]{1,0:T(8,128)(2,1)}, bf16[160,1536]{1,0:T(8,128)(2,1)S(1)}, u32[]{:S(2)}, u32[]{:S(2)}) collective-permute-start(bf16[160,1536]{1,0:T(8,128)(2,1)} %fusion.3), channel_id=1, source_target_pairs={{0,8},{8,16},{16,24},{24,0},{1,9},{9,17},{17,25},{25,1},{2,10},{10... | collective-permute-start | bytes 1474568 | tf_op jit(solution)/shard_map/ppermute | solution.py:30
  29.5 0.4 fusion.14
  29.9 1.2 %fusion.4 = bf16[160,1536]{1,0:T(8,128)(2,1)} fusion(f32[160,1536]{1,0:T(8,128)S(1)} %fusion.14, bf16[160,256]{1,0:T(8,128)(2,1)S(1)} %copy-done.10, bf16[1,1536,256]{2,1,0:T(8,128)(2,1)S(1)} %copy-done.1), kind=kOutput, calls=%fused_computation.12 | convolution fusion | flops 126320640 | bytes 2342912 | tf_op jit(solution)/shard_map/dot_general | solution.py:56
  31.1 1.9 %collective-permute-start.6 = (bf16[160,1536]{1,0:T(8,128)(2,1)}, bf16[160,1536]{1,0:T(8,128)(2,1)}, u32[]{:S(2)}, u32[]{:S(2)}) collective-permute-start(bf16[160,1536]{1,0:T(8,128)(2,1)} %fusion.4), channel_id=1, source_target_pairs={{0,24},{8,0},{16,8},{24,16},{1,25},{9,1},{17,9},{25,17},{2,26},{10... | collective-permute-start | bytes 1474568 | tf_op jit(solution)/shard_map/ppermute | solution.py:30
  33.1 0.5 add_multiply_fusion
  33.6 1.3 %fusion.20 = f32[160,1536]{1,0:T(8,128)S(1)} fusion(bf16[1,1536,256]{2,1,0:T(8,128)(2,1)S(1)} %copy-done, bf16[1,640,256]{2,1,0:T(8,128)(2,1)} %param.14, s32[]{:T(128)S(6)} %select_n.65), kind=kOutput, calls=%fused_computation.33 | convolution fusion | flops 125829120 | bytes 1851396 | tf_op jit(solution)/shard_map/dot_general | solution.py:54
  34.9 5.1 %collective-permute-done.5 = bf16[160,1536]{1,0:T(8,128)(2,1)S(1)} collective-permute-done((bf16[160,1536]{1,0:T(8,128)(2,1)}, bf16[160,1536]{1,0:T(8,128)(2,1)S(1)}, u32[]{:S(2)}, u32[]{:S(2)}) %collective-permute-start.5) | collective-permute-done | bytes 491552 | tf_op jit(solution)/shard_map/ppermute | solution.py:30
  40.0 6.6 %collective-permute-done.6 = bf16[160,1536]{1,0:T(8,128)(2,1)} collective-permute-done((bf16[160,1536]{1,0:T(8,128)(2,1)}, bf16[160,1536]{1,0:T(8,128)(2,1)}, u32[]{:S(2)}, u32[]{:S(2)}) %collective-permute-start.6) | collective-permute-done | bytes 491552 | tf_op jit(solution)/shard_map/ppermute | solution.py:30
  46.7 1.6 %add_convert_fusion = bf16[160,1536]{1,0:T(8,128)(2,1)S(1)} fusion(bf16[160,1536]{1,0:T(8,128)(2,1)} %collective-permute-done.6, bf16[160,1536]{1,0:T(8,128)(2,1)S(1)} %collective-permute-done.5, bf16[160,1536]{1,0:T(8,128)(2,1)S(1)} %collective-permute-done.4, f32[160,1536]{1,0:T(8,128)S(1)} %fusion.20, bf16[1,1536,256]{2,1,0:T(8,128)(2,1)S(1)} %copy-done.1, ...), kind=kOutput, calls=%fused_computation.18 | convolution fusion | flops 127795200 | bytes 3817476 | tf_op jit(solution)/shard_map/dot_general | solution.py:56
  48.2 1.9 %collective-permute-start.7 = (bf16[160,1536]{1,0:T(8,128)(2,1)S(1)}, bf16[160,1536]{1,0:T(8,128)(2,1)S(1)}, u32[]{:S(2)}, u32[]{:S(2)}) collective-permute-start(bf16[160,1536]{1,0:T(8,128)(2,1)S(1)} %add_convert_fusion), channel_id=1, source_target_pairs={{0,128},{128,0},{1,129},{129,1},{2,130},{130,2},{3,131},{131,3},{4... | collective-permute-start | bytes 1474568 | tf_op jit(solution)/shard_map/ppermute | solution.py:34
  50.2 0.7 fusion.56
  50.9 0.2 slice_reduce_fusion.1
  51.1 0.4 convolution_convert_fusion.2
  51.5 2.4 %collective-permute-start = (bf16[160,1536]{1,0:T(8,128)(2,1)S(1)}, bf16[160,1536]{1,0:T(8,128)(2,1)}, u32[]{:S(2)}, u32[]{:S(2)}) collective-permute-start(bf16[160,1536]{1,0:T(8,128)(2,1)S(1)} %convolution_convert_fusion.2), channel_id=1, source_target_pairs={{0,128},{128,0},{1,129},{129,1},{2,130},{130,2},{3,131},{131,3},{4... | collective-permute-start | bytes 1474568 | tf_op jit(solution)/shard_map/ppermute | solution.py:34
  54.0 0.3 fusion.40
  54.3 0.2 slice_reduce_fusion.3
  54.5 1.1 fusion.7
  55.5 11.7 %all-to-all-start.1 = ((bf16[16,8,1536]{2,1,0:T(8,128)(2,1)}), bf16[16,8,1536]{2,1,0:T(8,128)(2,1)S(1)}, u32[]{:S(2)}, u32[]{:S(2)}) async-start(bf16[16,8,1536]{2,1,0:T(8,128)(2,1)} %fusion.7), calls=%async_computation.1 | async-start | bytes 786432 | tf_op jit(solution)/shard_map/all_to_all | solution.py:16
  67.3 1.6 %multiply_reduce_fusion.3 = (f32[160]{0:T(256)S(1)}, bf16[160,1536]{1,0:T(8,128)(2,1)S(1)}) fusion(bf16[160,1536]{1,0:T(8,128)(2,1)} %collective-permute-done, bf16[128,1664]{1,0:T(8,128)(2,1)S(1)} %bitcast.60, s32[128]{0:T(128)S(1)} %get-tuple-element.4, s32[128]{0:T(128)S(1)} %get-tuple-element.3), kind=kOutput, calls=%fused_computation.22 | convolution fusion | flops 64204640 | bytes 1377920 | tf_op jit(solution)/shard_map/dot_general | solution.py:89
  68.8 0.0 copy-start.13
  68.9 2.1 %collective-permute-start.3 = (bf16[160,1536]{1,0:T(8,128)(2,1)S(1)}, bf16[160,1536]{1,0:T(8,128)(2,1)S(1)}, u32[]{:S(2)}, u32[]{:S(2)}) collective-permute-start(bf16[160,1536]{1,0:T(8,128)(2,1)S(1)} %get-tuple-element.22), channel_id=1, source_target_pairs={{0,16},{8,24},{16,0},{24,8},{1,17},{9,25},{17,1},{25,9},{2,18},{10... | collective-permute-start | bytes 1474568 | tf_op jit(solution)/shard_map/ppermute | solution.py:30
  71.0 2.3 %collective-permute-start.2 = (bf16[160,1536]{1,0:T(8,128)(2,1)S(1)}, bf16[160,1536]{1,0:T(8,128)(2,1)S(1)}, u32[]{:S(2)}, u32[]{:S(2)}) collective-permute-start(bf16[160,1536]{1,0:T(8,128)(2,1)S(1)} %get-tuple-element.22), channel_id=1, source_target_pairs={{0,24},{8,0},{16,8},{24,16},{1,25},{9,1},{17,9},{25,17},{2,26},{10... | collective-permute-start | bytes 1474568 | tf_op jit(solution)/shard_map/ppermute | solution.py:30
  73.3 4.8 %collective-permute-start.1 = (bf16[160,1536]{1,0:T(8,128)(2,1)S(1)}, bf16[160,1536]{1,0:T(8,128)(2,1)S(1)}, u32[]{:S(2)}, u32[]{:S(2)}) collective-permute-start(bf16[160,1536]{1,0:T(8,128)(2,1)S(1)} %get-tuple-element.22), channel_id=1, source_target_pairs={{0,8},{8,16},{16,24},{24,0},{1,9},{9,17},{17,25},{25,1},{2,10},{10... | collective-permute-start | bytes 1474568 | tf_op jit(solution)/shard_map/ppermute | solution.py:30
  78.0 8.5 %collective-permute-done.3 = bf16[160,1536]{1,0:T(8,128)(2,1)S(1)} collective-permute-done((bf16[160,1536]{1,0:T(8,128)(2,1)S(1)}, bf16[160,1536]{1,0:T(8,128)(2,1)S(1)}, u32[]{:S(2)}, u32[]{:S(2)}) %collective-permute-start.3) | collective-permute-done | bytes 491552 | tf_op jit(solution)/shard_map/ppermute | solution.py:30
  86.6 0.2 multiply_reduce_fusion
  86.8 9.1 %collective-permute-done.2 = bf16[160,1536]{1,0:T(8,128)(2,1)S(1)} collective-permute-done((bf16[160,1536]{1,0:T(8,128)(2,1)S(1)}, bf16[160,1536]{1,0:T(8,128)(2,1)S(1)}, u32[]{:S(2)}, u32[]{:S(2)}) %collective-permute-start.2) | collective-permute-done | bytes 491552 | tf_op jit(solution)/shard_map/ppermute | solution.py:30
  95.8 0.2 multiply_reduce_fusion.1
  96.0 0.2 multiply_reduce_fusion.2
  96.2 0.1 convert_reduce_fusion
  96.3 0.2 fusion.69
  96.5 0.1 concatenate.17
  96.6 9.6 %all_to_all.15 = f32[4,1,768]{2,1,0:T(1,128)S(1)} all-to-all(f32[4,1,768]{2,1,0:T(1,128)S(1)} %broadcast_in_dim.15), channel_id=1, replica_groups=mesh['zh'=2,'core'=2,'rep'=4,'x'=4,'zl'=8] {'rep'}, dimensions={0} | all-to-all | bytes 24576 | tf_op jit(solution)/shard_map/all_to_all | solution.py:16
  106.2 0.1 fusion.81
  106.3 0.7 fusion.73
  107.0 3.1 %fusion.1 = bf16[1,1536,256]{2,1,0:T(8,128)(2,1)} fusion(bf16[160,256]{1,0:T(8,128)(2,1)S(1)} %copy-done.9, bf16[160,256]{1,0:T(8,128)(2,1)S(1)} %copy-done.7, bf16[160,256]{1,0:T(8,128)(2,1)S(1)} %copy-done.11, bf16[160,256]{1,0:T(8,128)(2,1)S(1)} %copy-done.15, bf16[160,1536]{1,0:T(8,128)(2,1)S(1)} %collective-permute-done.3, ...), kind=kOutput, calls=%fused_computation.9 | convolution fusion | flops 515833856 | bytes 3088896 | tf_op jit(solution)/shard_map/dot_general | solution.py:138
  110.1 2.0 %fusion = bf16[1,1536,256]{2,1,0:T(8,128)(2,1)} fusion(bf16[160,256]{1,0:T(8,128)(2,1)S(1)} %copy-done.3, bf16[160,256]{1,0:T(8,128)(2,1)S(1)} %copy-done.5, bf16[160,256]{1,0:T(8,128)(2,1)S(1)} %get-tuple-element.23, bf16[160,256]{1,0:T(8,128)(2,1)S(1)} %copy-done.14, bf16[160,1536]{1,0:T(8,128)(2,1)S(1)} %collective-permute-done.3, ...), kind=kOutput, calls=%fused_computation.8 | convolution fusion | flops 515833856 | bytes 3088896 | tf_op jit(solution)/shard_map/dot_general | solution.py:135
  (50 shorter events, 0.2 us)
Async XLA Ops:
  0.6 2.0 %copy-start = (bf16[1,1536,256]{2,1,0:T(8,128)(2,1)S(1)}, bf16[1,1536,256]{2,1,0:T(8,128)(2,1)}, u32[]{:S(2)}) copy-start(bf16[1,1536,256]{2,1,0:T(8,128)(2,1)} %param.12) | copy-start | bytes 2359300
  2.6 0.6 copy-start.2
  2.6 1.7 %copy-start.8 = (bf16[160,256]{1,0:T(8,128)(2,1)}, bf16[160,256]{1,0:T(8,128)(2,1)S(1)}, u32[]{:S(2)}) copy-start(bf16[160,256]{1,0:T(8,128)(2,1)S(1)} %get-tuple-element.13) | copy-start | bytes 245764
  2.6 21.1 %copy-start.4 = (bf16[160,256]{1,0:T(8,128)(2,1)}, bf16[160,256]{1,0:T(8,128)(2,1)S(1)}, u32[]{:S(2)}) copy-start(bf16[160,256]{1,0:T(8,128)(2,1)S(1)} %get-tuple-element.25) | copy-start | bytes 245764
  2.6 21.6 %copy-start.6 = (bf16[160,256]{1,0:T(8,128)(2,1)}, bf16[160,256]{1,0:T(8,128)(2,1)S(1)}, u32[]{:S(2)}) copy-start(bf16[160,256]{1,0:T(8,128)(2,1)S(1)} %get-tuple-element.12) | copy-start | bytes 245764
  2.6 1.3 %copy-start.1 = (bf16[1,1536,256]{2,1,0:T(8,128)(2,1)S(1)}, bf16[1,1536,256]{2,1,0:T(8,128)(2,1)}, u32[]{:S(2)}) copy-start(bf16[1,1536,256]{2,1,0:T(8,128)(2,1)} %param.13) | copy-start | bytes 2359300
  3.9 3.7 %copy-start.17 = (s32[8,2]{0,1:T(2,128)S(1)}, s32[8,2]{0,1:T(2,128)}, u32[]{:S(2)}) copy-start(s32[8,2]{0,1:T(2,128)} %param.11) | copy-start | bytes 196
  3.9 3.8 %copy-start.18 = (s32[8,2]{0,1:T(2,128)S(1)}, s32[8,2]{0,1:T(2,128)}, u32[]{:S(2)}) copy-start(s32[8,2]{0,1:T(2,128)} %param.10) | copy-start | bytes 196
  3.9 3.9 %copy-start.12 = (bf16[8,1536]{1,0:T(8,128)(2,1)S(1)}, bf16[8,1536]{1,0:T(8,128)(2,1)}, u32[]{:S(2)}) copy-start(bf16[8,1536]{1,0:T(8,128)(2,1)} %param.8) | copy-start | bytes 73732
  4.3 30.6 %collective-permute-start.4 = (bf16[160,1536]{1,0:T(8,128)(2,1)S(1)}, bf16[160,1536]{1,0:T(8,128)(2,1)S(1)}, u32[]{:S(2)}, u32[]{:S(2)}) collective-permute-start(bf16[160,1536]{1,0:T(8,128)(2,1)S(1)} %fusion.2), channel_id=1, source_target_pairs={{0,16},{8,24},{16,0},{24,8},{1,17},{9,25},{17,1},{25,9},{2,18},{10... | collective-permute-start | bytes 1474568 | tf_op jit(solution)/shard_map/ppermute | solution.py:30
  8.6 41.6 %all-to-all-start = ((bf16[16,8,1664]{2,1,0:T(8,128)(2,1)}), bf16[16,8,1664]{2,1,0:T(8,128)(2,1)S(1)}, u32[]{:S(2)}, u32[]{:S(2)}) async-start(bf16[16,8,1664]{2,1,0:T(8,128)(2,1)} %broadcast_in_dim.13), calls=%async_computation | async-start | bytes 851968 | tf_op jit(solution)/shard_map/all_to_all | solution.py:16
  25.4 4.5 %copy-start.10 = (bf16[160,256]{1,0:T(8,128)(2,1)S(1)}, bf16[160,256]{1,0:T(8,128)(2,1)}, u32[]{:S(2)}) copy-start(bf16[160,256]{1,0:T(8,128)(2,1)} %get-tuple-element.14) | copy-start | bytes 245764
  25.4 14.6 %collective-permute-start.5 = (bf16[160,1536]{1,0:T(8,128)(2,1)}, bf16[160,1536]{1,0:T(8,128)(2,1)S(1)}, u32[]{:S(2)}, u32[]{:S(2)}) collective-permute-start(bf16[160,1536]{1,0:T(8,128)(2,1)} %fusion.3), channel_id=1, source_target_pairs={{0,8},{8,16},{16,24},{24,0},{1,9},{9,17},{17,25},{25,1},{2,10},{10... | collective-permute-start | bytes 1474568 | tf_op jit(solution)/shard_map/ppermute | solution.py:30
  31.1 15.5 %collective-permute-start.6 = (bf16[160,1536]{1,0:T(8,128)(2,1)}, bf16[160,1536]{1,0:T(8,128)(2,1)}, u32[]{:S(2)}, u32[]{:S(2)}) collective-permute-start(bf16[160,1536]{1,0:T(8,128)(2,1)} %fusion.4), channel_id=1, source_target_pairs={{0,24},{8,0},{16,8},{24,16},{1,25},{9,1},{17,9},{25,17},{2,26},{10... | collective-permute-start | bytes 1474568 | tf_op jit(solution)/shard_map/ppermute | solution.py:30
  48.2 5.7 %collective-permute-start.7 = (bf16[160,1536]{1,0:T(8,128)(2,1)S(1)}, bf16[160,1536]{1,0:T(8,128)(2,1)S(1)}, u32[]{:S(2)}, u32[]{:S(2)}) collective-permute-start(bf16[160,1536]{1,0:T(8,128)(2,1)S(1)} %add_convert_fusion), channel_id=1, source_target_pairs={{0,128},{128,0},{1,129},{129,1},{2,130},{130,2},{3,131},{131,3},{4... | collective-permute-start | bytes 1474568 | tf_op jit(solution)/shard_map/ppermute | solution.py:34
  51.5 15.7 %collective-permute-start = (bf16[160,1536]{1,0:T(8,128)(2,1)S(1)}, bf16[160,1536]{1,0:T(8,128)(2,1)}, u32[]{:S(2)}, u32[]{:S(2)}) collective-permute-start(bf16[160,1536]{1,0:T(8,128)(2,1)S(1)} %convolution_convert_fusion.2), channel_id=1, source_target_pairs={{0,128},{128,0},{1,129},{129,1},{2,130},{130,2},{3,131},{131,3},{4... | collective-permute-start | bytes 1474568 | tf_op jit(solution)/shard_map/ppermute | solution.py:34
  55.5 40.7 %all-to-all-start.1 = ((bf16[16,8,1536]{2,1,0:T(8,128)(2,1)}), bf16[16,8,1536]{2,1,0:T(8,128)(2,1)S(1)}, u32[]{:S(2)}, u32[]{:S(2)}) async-start(bf16[16,8,1536]{2,1,0:T(8,128)(2,1)} %fusion.7), calls=%async_computation.1 | async-start | bytes 786432 | tf_op jit(solution)/shard_map/all_to_all | solution.py:16
  68.8 27.2 %copy-start.19 = (bf16[160,1536]{1,0:T(8,128)(2,1)}, bf16[160,1536]{1,0:T(8,128)(2,1)S(1)}, u32[]{:S(2)}) copy-start(bf16[160,1536]{1,0:T(8,128)(2,1)S(1)} %get-tuple-element.22) | copy-start | bytes 1474564
  68.8 27.4 %copy-start.13 = (bf16[8,1536]{1,0:T(8,128)(2,1)S(1)}, bf16[8,1536]{1,0:T(8,128)(2,1)}, u32[]{:S(2)}) copy-start(bf16[8,1536]{1,0:T(8,128)(2,1)} %param.8) | copy-start | bytes 73732
  68.9 27.4 %copy-start.16 = (f32[1536]{0:T(1024)S(1)}, f32[1536]{0:T(1024)}, u32[]{:S(2)}) copy-start(f32[1536]{0:T(1024)} %param.9) | copy-start | bytes 18436
  68.9 38.1 %copy-start.7 = (bf16[160,256]{1,0:T(8,128)(2,1)S(1)}, bf16[160,256]{1,0:T(8,128)(2,1)}, u32[]{:S(2)}) copy-start(bf16[160,256]{1,0:T(8,128)(2,1)} %copy-done.6) | copy-start | bytes 245764
  68.9 38.1 %copy-start.9 = (bf16[160,256]{1,0:T(8,128)(2,1)S(1)}, bf16[160,256]{1,0:T(8,128)(2,1)}, u32[]{:S(2)}) copy-start(bf16[160,256]{1,0:T(8,128)(2,1)} %copy-done.8) | copy-start | bytes 245764
  68.9 38.1 %copy-start.11 = (bf16[160,256]{1,0:T(8,128)(2,1)S(1)}, bf16[160,256]{1,0:T(8,128)(2,1)}, u32[]{:S(2)}) copy-start(bf16[160,256]{1,0:T(8,128)(2,1)} %get-tuple-element.14) | copy-start | bytes 245764
  68.9 38.1 %copy-start.15 = (bf16[160,256]{1,0:T(8,128)(2,1)S(1)}, bf16[160,256]{1,0:T(8,128)(2,1)}, u32[]{:S(2)}) copy-start(bf16[160,256]{1,0:T(8,128)(2,1)} %get-tuple-element.11) | copy-start | bytes 245764
  68.9 17.7 %collective-permute-start.3 = (bf16[160,1536]{1,0:T(8,128)(2,1)S(1)}, bf16[160,1536]{1,0:T(8,128)(2,1)S(1)}, u32[]{:S(2)}, u32[]{:S(2)}) collective-permute-start(bf16[160,1536]{1,0:T(8,128)(2,1)S(1)} %get-tuple-element.22), channel_id=1, source_target_pairs={{0,16},{8,24},{16,0},{24,8},{1,17},{9,25},{17,1},{25,9},{2,18},{10... | collective-permute-start | bytes 1474568 | tf_op jit(solution)/shard_map/ppermute | solution.py:30
  71.0 24.9 %collective-permute-start.2 = (bf16[160,1536]{1,0:T(8,128)(2,1)S(1)}, bf16[160,1536]{1,0:T(8,128)(2,1)S(1)}, u32[]{:S(2)}, u32[]{:S(2)}) collective-permute-start(bf16[160,1536]{1,0:T(8,128)(2,1)S(1)} %get-tuple-element.22), channel_id=1, source_target_pairs={{0,24},{8,0},{16,8},{24,16},{1,25},{9,1},{17,9},{25,17},{2,26},{10... | collective-permute-start | bytes 1474568 | tf_op jit(solution)/shard_map/ppermute | solution.py:30
  73.3 22.7 %collective-permute-start.1 = (bf16[160,1536]{1,0:T(8,128)(2,1)S(1)}, bf16[160,1536]{1,0:T(8,128)(2,1)S(1)}, u32[]{:S(2)}, u32[]{:S(2)}) collective-permute-start(bf16[160,1536]{1,0:T(8,128)(2,1)S(1)} %get-tuple-element.22), channel_id=1, source_target_pairs={{0,8},{8,16},{16,24},{24,0},{1,9},{9,17},{17,25},{25,1},{2,10},{10... | collective-permute-start | bytes 1474568 | tf_op jit(solution)/shard_map/ppermute | solution.py:30
  107.0 3.1 %copy-start.3 = (bf16[160,256]{1,0:T(8,128)(2,1)S(1)}, bf16[160,256]{1,0:T(8,128)(2,1)}, u32[]{:S(2)}) copy-start(bf16[160,256]{1,0:T(8,128)(2,1)} %copy-done.2) | copy-start | bytes 245764
  107.0 3.1 %copy-start.5 = (bf16[160,256]{1,0:T(8,128)(2,1)S(1)}, bf16[160,256]{1,0:T(8,128)(2,1)}, u32[]{:S(2)}) copy-start(bf16[160,256]{1,0:T(8,128)(2,1)} %copy-done.4) | copy-start | bytes 245764
  107.0 3.1 %copy-start.14 = (bf16[160,256]{1,0:T(8,128)(2,1)S(1)}, bf16[160,256]{1,0:T(8,128)(2,1)}, u32[]{:S(2)}) copy-start(bf16[160,256]{1,0:T(8,128)(2,1)} %get-tuple-element.26) | copy-start | bytes 245764
  107.0 3.1 %copy-start.20 = (bf16[160,1536]{1,0:T(8,128)(2,1)S(1)}, bf16[160,1536]{1,0:T(8,128)(2,1)}, u32[]{:S(2)}) copy-start(bf16[160,1536]{1,0:T(8,128)(2,1)} %copy-done.19) | copy-start | bytes 1474564
